TPU v7x, 256 devices: a whole 4x4x8 slice. The times are simulated.
256 devices in a mesh: row: 32 (over x_hi, z, core), feat: 8 (over y, x_lo).
Axes of the slice: x: 4 (x_hi: 2, x_lo: 2; x = x_hi * 2 + x_lo), y: 4, z: 8, core: 2. Of those that a mesh axis runs over, the one named last changes fastest.
Arguments:
- bin_index: int32 [1024, 98304], P('feat', 'row'), may hold values from 0 to 63
- gradient: bfloat16 [32, 98304], P(None, ('row', 'feat')), may hold values from -6 to 6
- hessian: bfloat16 [98304], P(('row', 'feat')), may hold values from 0.25 to 4
- row_node: int32 [98304], P('row'), may hold values from 0 to 7
Outputs:
- split_gain: float32 [1024, 512], P(('feat', 'row'))
- best_gain: float32 [8], replicated
All inputs are finite; a program needn't handle non-finite values.
Results may differ from a plain program's by a relative error of at most 0.0003.
Values may be sent and summed in bfloat16 or wider, within the bound.
No kernel may reach another device: no remote copies, remote signals or barrier semaphores. Data moves between devices by JAX's collectives and lax.ppermute only.
A program may use at most 128 MiB of HBM per device.

v0:
```python
import functools
import math
import jax
import jax.numpy as jnp
from jax import lax
from jax.sharding import Mesh
from jax.sharding import PartitionSpec as P

BINS = 64
NODES = 8
ROW = ("row_0", "row_1", "row_2")
FEAT = ("feat_0", "feat_1")
ROW_FEAT = ("row_0", "row_1", "row_2", "feat_0", "feat_1")
FEAT_ROW = ("feat_0", "feat_1", "row_0", "row_1", "row_2")
ridge_term = 1.0


def by_axis(x, axes):
    return functools.reduce(lax.psum, axes, x)


def gather_turned(arrays, axis, dims):
    turned = [jnp.moveaxis(a, dim, 0) for a, dim in zip(arrays, dims)]
    both = jnp.concatenate([t.reshape(len(t), -1) for t in turned], axis=1)
    result, at, gathered = (lax.all_gather(both, axis, axis=0, tiled=True), 0, [])
    for t, dim in zip(turned, dims):
        section = result[:, at : at + t[0].size].reshape(-1, *t.shape[1:])
        gathered.append(jnp.moveaxis(section, 0, dim))
        at += t[0].size
    return tuple(gathered)


def one_axis_at_a_time(x, axes):
    for axis in axes:
        x = lax.pmax(x, axis)
    return x


def masked_rows(node_ids, grad_rows, hess_rows):
    stacked = jnp.concatenate([grad_rows, hess_rows[None, :]], 0)
    picked = (node_ids[None, :] == jnp.arange(NODES, dtype=jnp.int32)[:, None]).astype(jnp.bfloat16)
    return (picked[:, None, :] * stacked[None, :, :]).reshape(-1, node_ids.shape[0])


def histogram_block(feature_block, masked):
    levels = jnp.arange(BINS, dtype=jnp.int32)
    onehot = (feature_block[:, None, :] == levels[None, :, None]).astype(jnp.bfloat16)
    return jnp.einsum("fbr,mr->fbm", onehot, masked, preferred_element_type=jnp.float32)


def score_splits(histogram, node_totals):
    left_sums = jnp.cumsum(histogram, axis=1)
    whole_sums = node_totals[None, None]
    right_sums = whole_sums - left_sums

    def part_score(sums):
        return jnp.sum(sums[..., :-1] * sums[..., :-1], axis=-1) / (sums[..., -1] + ridge_term)

    outputs_count = histogram.shape[-1] - 1
    score_terms = part_score(left_sums) + part_score(right_sums) - part_score(whole_sums)
    return jnp.transpose(0.5 / outputs_count * score_terms, (0, 2, 1))


def on_device(bin_index, gradient, hessian, row_node):
    local_features = bin_index.shape[0]
    owned_count = local_features // lax.axis_size(ROW)
    outputs_count = gradient.shape[0]
    shard_rows = gradient.shape[1]
    first_local = lax.axis_index(FEAT) * shard_rows
    local_nodes = lax.dynamic_slice_in_dim(row_node, first_local, shard_rows, 0)
    stacked = jnp.concatenate([gradient, hessian[None, :]], 0)
    picked = (local_nodes[None, :] == jnp.arange(NODES, dtype=jnp.int32)[:, None]).astype(
        jnp.bfloat16
    )
    local_totals = jnp.einsum("nr,mr->nm", picked, stacked, preferred_element_type=jnp.float32)
    node_totals = by_axis(local_totals, ROW_FEAT)
    grad_rows, hess_rows = gather_turned((gradient, hessian), FEAT, (1, 0))
    masked = masked_rows(row_node, grad_rows, hess_rows)
    group_size = math.gcd(owned_count * lax.axis_size(ROW), 16)

    def one_group(step_index):
        feature_block = lax.dynamic_slice_in_dim(bin_index, step_index * group_size, group_size, 0)
        return histogram_block(feature_block, masked).reshape(group_size, -1)

    pieces = lax.map(
        one_group, jnp.arange(owned_count * lax.axis_size(ROW) // group_size, dtype=jnp.int32)
    )
    owned = lax.psum_scatter(
        pieces.reshape(owned_count * lax.axis_size(ROW), -1), ROW, scatter_dimension=0, tiled=True
    )
    histogram = owned.reshape(owned_count, BINS, NODES, outputs_count + 1)
    split_gain = score_splits(histogram, node_totals)
    best_gain = one_axis_at_a_time(jnp.max(split_gain, axis=(0, 2)), ROW_FEAT)
    return (split_gain.reshape(owned_count, NODES * BINS), best_gain)


def solution(mesh):
    split = Mesh(
        mesh.devices.reshape(2, 8, 2, 4, 2), ("row_0", "row_1", "row_2", "feat_0", "feat_1")
    )
    in_specs = (P(FEAT, ROW), P(None, ROW_FEAT), P(ROW_FEAT), P(ROW))
    out_specs = (P(FEAT_ROW, None), P())
    return jax.shard_map(
        on_device, mesh=split, in_specs=in_specs, out_specs=out_specs, check_vma=False
    )
```

profile of v0, /device:TPU:32, one launch (start us, length us, event | category | flops | bytes accessed | tf_op | source)
XLA Modules:
  0.0 494.6 jit_solution(4943222124883276265)
XLA Ops:
  8.6 29.1 %all_gather.3 = bf16[3072,33]{0,1:T(8,128)(2,1)S(1)} all-gather(bf16[384,33]{0,1:T(8,128)(2,1)S(1)} %pad_maximum_fusion.1), channel_id=1, replica_groups=mesh['row_0'=2,'row_1'=8,'row_2'=2,'feat_0'=4,'feat_1'=2] {'feat_0','fea..., dimensions={0}, use_global_device_ids=true | all-gather | bytes 228096 | tf_op jit(solution)/shard_map/all_gather | solution.py:25
  38.5 86.3 %while.11 = (s32[]{:T(128)}, f32[8,16,16896]{2,1,0:T(8,128)}, s32[8]{0:T(128)S(1)}, s32[128,3072]{1,0:T(8,128)}, bf16[33,3072]{1,0:T(8,128)(2,1)S(1)}, /*index=5...) while((s32[]{:T(128)}, f32[8,16,16896]{2,1,0:T(8,128)}, ...), condition=%wide.region_1.0_spmd.clone, body=%wide.region_0.0_spmd.clone.sunk | while | flops 1664901120 | bytes 12736687 | solution.py:85
  38.7 1.7 reshape.73
  42.6 4.8 fusion.28
  48.2 1.1 constant_dynamic-update-slice_fusion.2
  49.5 1.7 reshape.73
  53.4 4.8 fusion.28
  60.3 1.7 reshape.73
  64.2 4.8 fusion.28
  71.1 1.7 reshape.73
  75.0 4.8 fusion.28
  81.8 1.7 reshape.73
  85.8 4.8 fusion.28
  92.7 1.7 reshape.73
  96.6 4.8 fusion.28
  103.4 1.7 reshape.73
  107.3 4.8 fusion.28
  114.2 1.7 reshape.73
  118.1 4.8 fusion.28
  126.4 6.4 %psum.35 = f32[8,33]{1,0:T(8,128)S(1)} all-reduce(f32[8,33]{1,0:T(8,128)S(1)} %fusion.7), channel_id=1, replica_groups=mesh['row_0'=2,'row_1'=8,'row_2'=2,'feat_0'=4,'feat_1'=2] {'row_0'}, use_global_device_ids=true, to_apply=%region_5.6 | all-reduce | flops 264 | bytes 2112 | tf_op jit(solution)/shard_map/psum | solution.py:19
  132.8 17.9 %psum.36 = f32[8,33]{1,0:T(8,128)S(1)} all-reduce(f32[8,33]{1,0:T(8,128)S(1)} %psum.35), channel_id=1, replica_groups=mesh['row_0'=2,'row_1'=8,'row_2'=2,'feat_0'=4,'feat_1'=2] {'row_1'}, use_global_device_ids=true, to_apply=%region_6.7 | all-reduce | flops 264 | bytes 2112 | tf_op jit(solution)/shard_map/psum | solution.py:19
  150.7 2.5 psum.37
  153.2 8.3 %psum.38 = f32[8,33]{1,0:T(8,128)S(1)} all-reduce(f32[8,33]{1,0:T(8,128)S(1)} %psum.37), channel_id=1, replica_groups=mesh['row_0'=2,'row_1'=8,'row_2'=2,'feat_0'=4,'feat_1'=2] {'feat_0'}, use_global_device_ids=true, to_apply=%region_8.9 | all-reduce | flops 264 | bytes 2112 | tf_op jit(solution)/shard_map/psum | solution.py:19
  161.5 6.6 %psum.39 = f32[8,33]{1,0:T(8,128)S(1)} all-reduce(f32[8,33]{1,0:T(8,128)S(1)} %psum.38), channel_id=1, replica_groups=mesh['row_0'=2,'row_1'=8,'row_2'=2,'feat_0'=4,'feat_1'=2] {'feat_1'}, use_global_device_ids=true, to_apply=%region_9.10 | all-reduce | flops 264 | bytes 2112 | tf_op jit(solution)/shard_map/psum | solution.py:19
  169.7 243.3 %all-reduce.3.cloned.1.call-done = f32[128,16896]{1,0:T(8,128)} async-done(((f32[128,16896]{1,0:T(8,128)}), f32[128,16896]{1,0:T(8,128)}) %all-reduce.3.cloned.1.call-update) | async-done | bytes 8650768
  414.1 1.2 reshape.66
  415.3 25.9 %fusion.22 = f32[4,64,8,33]{3,2,1,0:T(8,128)S(1)} fusion(f32[4,64,8,33]{3,2,1,0:T(8,128)S(1)} %reshape.66), kind=kOutput, calls=%fused_computation.38 | output fusion | flops 4257792 | bytes 540672 | tf_op jit(solution)/shard_map/jit(cumsum)/reduce_window_sum | solution.py:52
  442.4 6.4 %pmax.35 = f32[8]{0:T(128)S(1)} all-reduce(f32[8]{0:T(128)S(1)} %get-tuple-element.58), channel_id=1, replica_groups=mesh['row_0'=2,'row_1'=8,'row_2'=2,'feat_0'=4,'feat_1'=2] {'row_0'}, use_global_device_ids=true, to_apply=%region_13.14 | all-reduce | flops 8 | bytes 64 | tf_op jit(solution)/shard_map/pmax | solution.py:35
  448.8 19.9 %pmax.36 = f32[8]{0:T(128)S(1)} all-reduce(f32[8]{0:T(128)S(1)} %pmax.35), channel_id=1, replica_groups=mesh['row_0'=2,'row_1'=8,'row_2'=2,'feat_0'=4,'feat_1'=2] {'row_1'}, use_global_device_ids=true, to_apply=%region_14.15 | all-reduce | flops 8 | bytes 64 | tf_op jit(solution)/shard_map/pmax | solution.py:35
  468.8 2.5 pmax.37
  471.2 10.4 %pmax.38 = f32[8]{0:T(128)S(1)} all-reduce(f32[8]{0:T(128)S(1)} %pmax.37), channel_id=1, replica_groups=mesh['row_0'=2,'row_1'=8,'row_2'=2,'feat_0'=4,'feat_1'=2] {'feat_0'}, use_global_device_ids=true, to_apply=%region_16.17 | all-reduce | flops 8 | bytes 64 | tf_op jit(solution)/shard_map/pmax | solution.py:35
  482.4 5.4 %pmax.39 = f32[8]{0:T(128)} all-reduce(f32[8]{0:T(128)S(1)} %pmax.38), channel_id=1, replica_groups=mesh['row_0'=2,'row_1'=8,'row_2'=2,'feat_0'=4,'feat_1'=2] {'feat_1'}, use_global_device_ids=true, to_apply=%region_17.18 | all-reduce | flops 8 | bytes 64 | tf_op jit(solution)/shard_map/pmax | solution.py:35
  (71 shorter events, 35.0 us)
Async XLA Ops:
  7.2 405.9 %all-reduce.3.cloned.1.call-start = ((), (), s32[]{:S(2)}) async-start(), calls=%async_computation | async-start | bytes 17301504
  124.8 0.7 copy-start.1
  124.8 1.5 copy-start
  124.8 43.7 %copy-start.2 = (u32[256]{0:T(256)S(1)}, u32[256]{0:T(256)}, u32[]{:S(2)}) copy-start(u32[256]{0:T(256)} %constant.46) | copy-start | bytes 3076
Sparse Core Ops, SparseCore 0:
  125.0 287.9 all-reduce.2
where the time goes:
time: 496 us; the launch traced here: 495 us
  waiting for transfers between devices  243 us (49%)
  blocking collectives  115 us (23%)
  local copies, waits for them, and re-layouts  47.1 us (9%)
  matrix products  38.9 us (8%)
  other arithmetic  29.7 us (6%)
  between operations  14.8 us (3%)
  loops' own time  5.37 us (1%)
    unnamed x2, waiting for transfers between devices  243 us
    pmax x5, blocking collectives, one_axis_at_a_time(): x = lax.pmax(x, axis)  44.7 us
    psum x5, blocking collectives, by_axis(): return functools.reduce(lax.psum, axes, x)  41.7 us
    dot_general x8, matrix products, histogram_block(): jnp.einsum('fbr,mr->fbm', onehot, masked, preferred_element_type=jnp.floa...  38.8 us
    all_gather x1, blocking collectives, gather_turned(): lax.all_gather(both, axis, axis=0, tiled=True)  29.1 us
    another operation x1, other arithmetic, score_splits(): left_sums = jnp.cumsum(histogram, axis=1)  25.9 us
    mul x8, local copies, waits for them, and re-layouts, masked_rows(): picked[:, None, :] * stacked[None, :, :]  13.8 us
  transfers between devices with their start and end apart: 1, of which 1 were waited for; matrix products, arithmetic and copies ran while one was open for 0% of the time, Pallas kernels for 0%

commit v1 on v0

--- a/solution.py
+++ b/solution.py
@@ -15,6 +15,13 @@
 ridge_term = 1.0
 
 
+def gather_over(value, mesh_axis, dim):
+    count = lax.axis_size(mesh_axis)
+    blocks = jnp.stack([value for _ in range(count)])
+    blocks = lax.all_to_all(blocks, mesh_axis, split_axis=0, concat_axis=0)
+    return jnp.concatenate(blocks, axis=dim)
+
+
 def by_axis(x, axes):
     return functools.reduce(lax.psum, axes, x)
 
@@ -22,7 +29,7 @@
 def gather_turned(arrays, axis, dims):
     turned = [jnp.moveaxis(a, dim, 0) for a, dim in zip(arrays, dims)]
     both = jnp.concatenate([t.reshape(len(t), -1) for t in turned], axis=1)
-    result, at, gathered = (lax.all_gather(both, axis, axis=0, tiled=True), 0, [])
+    result, at, gathered = (gather_over(both, axis, 0), 0, [])
     for t, dim in zip(turned, dims):
         section = result[:, at : at + t[0].size].reshape(-1, *t.shape[1:])
         gathered.append(jnp.moveaxis(section, 0, dim))

time: 496 us -> 478 us (0.964)
  blocking collectives: 115 us -> 85 us
  waiting for transfers between devices: 243 us -> 250 us
  starting transfers between devices: 0.04 us -> 5.43 us
    all_gather x1 -> x0, blocking collectives: 29.1 us -> none  [gather_turned(): lax.all_gather(both, axis, axis=0, tiled=True)]
    all_to_all x0 -> x1, waiting for transfers between devices: none -> 6.42 us  [gather_over(): blocks = lax.all_to_all(blocks, mesh_axis, split_axis=0, concat_axis=0)]
    all_to_all x0 -> x1, starting transfers between devices: none -> 5.4 us  [gather_over(): blocks = lax.all_to_all(blocks, mesh_axis, split_axis=0, concat_axis=0)]
  transfers between devices with their start and end apart: 1 -> 2, of which waited for: 1 -> 2; matrix products, arithmetic and copies ran while one was open for 0% -> 1% of each run, Pallas kernels for 0% -> 0%
where the time goes in v1:
time: 478 us; the launch traced here: 477 us
  waiting for transfers between devices  250 us (52%)
  blocking collectives  85 us (18%)
  local copies, waits for them, and re-layouts  48.1 us (10%)
  matrix products  38.9 us (8%)
  other arithmetic  29.7 us (6%)
  between operations  14.8 us (3%)
  starting transfers between devices  5.43 us (1%)
  loops' own time  5.37 us (1%)
    unnamed x2, waiting for transfers between devices  243 us
    pmax x5, blocking collectives, one_axis_at_a_time(): x = lax.pmax(x, axis)  44.7 us
    psum x5, blocking collectives, by_axis(): return functools.reduce(lax.psum, axes, x)  40.3 us
    dot_general x8, matrix products, histogram_block(): jnp.einsum('fbr,mr->fbm', onehot, masked, preferred_element_type=jnp.floa...  38.8 us
    another operation x1, other arithmetic, score_splits(): left_sums = jnp.cumsum(histogram, axis=1)  25.9 us
    mul x8, local copies, waits for them, and re-layouts, masked_rows(): picked[:, None, :] * stacked[None, :, :]  14.1 us
  transfers between devices with their start and end apart: 2, of which 2 were waited for; matrix products, arithmetic and copies ran while one was open for 1% of the time, Pallas kernels for 0%

profile of v1, /device:TPU:32, one launch (start us, length us, event | category | flops | bytes accessed | tf_op | source)
XLA Modules:
  0.0 477.0 jit_solution(6063569724686855559)
XLA Ops:
  9.3 5.4 %all-to-all-start = ((bf16[8,384,33]{1,2,0:T(8,128)(2,1)}), bf16[8,384,33]{1,2,0:T(8,128)(2,1)S(1)}, u32[]{:S(2)}, u32[]{:S(2)}) async-start(bf16[8,384,33]{1,2,0:T(8,128)(2,1)} %stack.2), calls=%async_computation | async-start | bytes 491520 | tf_op jit(solution)/shard_map/all_to_all | solution.py:21
  15.5 6.4 %all-to-all-done = bf16[8,384,33]{1,2,0:T(8,128)(2,1)S(1)} async-done(((bf16[8,384,33]{1,2,0:T(8,128)(2,1)}), bf16[8,384,33]{1,2,0:T(8,128)(2,1)S(1)}, u32[]{:S(2)}, u32[]{:S(2)}) %all-to-all-start) | async-done | bytes 202784 | tf_op jit(solution)/shard_map/all_to_all | solution.py:21
  22.1 86.5 %while.11 = (s32[]{:T(128)}, f32[8,16,16896]{2,1,0:T(8,128)}, s32[8]{0:T(128)S(1)}, s32[128,3072]{1,0:T(8,128)}, bf16[33,3072]{1,0:T(8,128)(2,1)S(1)}, /*index=5...) while((s32[]{:T(128)}, f32[8,16,16896]{2,1,0:T(8,128)}, ...), condition=%wide.region_1.0_spmd.clone, body=%wide.region_0.0_spmd.clone.sunk | while | flops 1664901120 | bytes 12736687 | solution.py:92
  22.3 1.8 reshape.79
  26.2 4.8 %fusion.28 = f32[16,64,264]{2,1,0:T(8,128)S(1)} fusion(bf16[264,3072,1]{1,0,2:T(8,128)(2,1)} %reshape.79, s32[16,3072]{1,0:T(8,128)S(1)} %constant_dynamic-slice_fusion.3), kind=kOutput, calls=%fused_computation.2.clone.1 | convolution fusion | flops 1664090112 | bytes 2899968 | tf_op jit(solution)/shard_map/while/body/eval_jaxpr/fbr,mr->fbm/dot_general | solution.py:55
  33.1 1.8 reshape.79
  37.0 4.8 %fusion.28 = f32[16,64,264]{2,1,0:T(8,128)S(1)} fusion(bf16[264,3072,1]{1,0,2:T(8,128)(2,1)} %reshape.79, s32[16,3072]{1,0:T(8,128)S(1)} %constant_dynamic-slice_fusion.3), kind=kOutput, calls=%fused_computation.2.clone.1 | convolution fusion | flops 1664090112 | bytes 2899968 | tf_op jit(solution)/shard_map/while/body/eval_jaxpr/fbr,mr->fbm/dot_general | solution.py:55
  43.9 1.8 reshape.79
  47.9 4.8 %fusion.28 = f32[16,64,264]{2,1,0:T(8,128)S(1)} fusion(bf16[264,3072,1]{1,0,2:T(8,128)(2,1)} %reshape.79, s32[16,3072]{1,0:T(8,128)S(1)} %constant_dynamic-slice_fusion.3), kind=kOutput, calls=%fused_computation.2.clone.1 | convolution fusion | flops 1664090112 | bytes 2899968 | tf_op jit(solution)/shard_map/while/body/eval_jaxpr/fbr,mr->fbm/dot_general | solution.py:55
  54.7 1.8 reshape.79
  58.7 4.8 %fusion.28 = f32[16,64,264]{2,1,0:T(8,128)S(1)} fusion(bf16[264,3072,1]{1,0,2:T(8,128)(2,1)} %reshape.79, s32[16,3072]{1,0:T(8,128)S(1)} %constant_dynamic-slice_fusion.3), kind=kOutput, calls=%fused_computation.2.clone.1 | convolution fusion | flops 1664090112 | bytes 2899968 | tf_op jit(solution)/shard_map/while/body/eval_jaxpr/fbr,mr->fbm/dot_general | solution.py:55
  65.5 1.8 reshape.79
  69.5 4.8 %fusion.28 = f32[16,64,264]{2,1,0:T(8,128)S(1)} fusion(bf16[264,3072,1]{1,0,2:T(8,128)(2,1)} %reshape.79, s32[16,3072]{1,0:T(8,128)S(1)} %constant_dynamic-slice_fusion.3), kind=kOutput, calls=%fused_computation.2.clone.1 | convolution fusion | flops 1664090112 | bytes 2899968 | tf_op jit(solution)/shard_map/while/body/eval_jaxpr/fbr,mr->fbm/dot_general | solution.py:55
  76.3 1.8 reshape.79
  80.3 4.8 %fusion.28 = f32[16,64,264]{2,1,0:T(8,128)S(1)} fusion(bf16[264,3072,1]{1,0,2:T(8,128)(2,1)} %reshape.79, s32[16,3072]{1,0:T(8,128)S(1)} %constant_dynamic-slice_fusion.3), kind=kOutput, calls=%fused_computation.2.clone.1 | convolution fusion | flops 1664090112 | bytes 2899968 | tf_op jit(solution)/shard_map/while/body/eval_jaxpr/fbr,mr->fbm/dot_general | solution.py:55
  87.1 1.8 reshape.79
  91.1 4.8 %fusion.28 = f32[16,64,264]{2,1,0:T(8,128)S(1)} fusion(bf16[264,3072,1]{1,0,2:T(8,128)(2,1)} %reshape.79, s32[16,3072]{1,0:T(8,128)S(1)} %constant_dynamic-slice_fusion.3), kind=kOutput, calls=%fused_computation.2.clone.1 | convolution fusion | flops 1664090112 | bytes 2899968 | tf_op jit(solution)/shard_map/while/body/eval_jaxpr/fbr,mr->fbm/dot_general | solution.py:55
  98.0 1.8 reshape.79
  101.9 4.8 %fusion.28 = f32[16,64,264]{2,1,0:T(8,128)S(1)} fusion(bf16[264,3072,1]{1,0,2:T(8,128)(2,1)} %reshape.79, s32[16,3072]{1,0:T(8,128)S(1)} %constant_dynamic-slice_fusion.3), kind=kOutput, calls=%fused_computation.2.clone.1 | convolution fusion | flops 1664090112 | bytes 2899968 | tf_op jit(solution)/shard_map/while/body/eval_jaxpr/fbr,mr->fbm/dot_general | solution.py:55
  110.2 6.4 %psum.35 = f32[8,33]{1,0:T(8,128)S(1)} all-reduce(f32[8,33]{1,0:T(8,128)S(1)} %fusion.7), channel_id=1, replica_groups=mesh['row_0'=2,'row_1'=8,'row_2'=2,'feat_0'=4,'feat_1'=2] {'row_0'}, use_global_device_ids=true, to_apply=%region_5.6 | all-reduce | flops 264 | bytes 2112 | tf_op jit(solution)/shard_map/psum | solution.py:26
  116.6 17.9 %psum.36 = f32[8,33]{1,0:T(8,128)S(1)} all-reduce(f32[8,33]{1,0:T(8,128)S(1)} %psum.35), channel_id=1, replica_groups=mesh['row_0'=2,'row_1'=8,'row_2'=2,'feat_0'=4,'feat_1'=2] {'row_1'}, use_global_device_ids=true, to_apply=%region_6.7 | all-reduce | flops 264 | bytes 2112 | tf_op jit(solution)/shard_map/psum | solution.py:26
  134.5 2.5 psum.37
  137.0 8.6 %psum.38 = f32[8,33]{1,0:T(8,128)S(1)} all-reduce(f32[8,33]{1,0:T(8,128)S(1)} %psum.37), channel_id=1, replica_groups=mesh['row_0'=2,'row_1'=8,'row_2'=2,'feat_0'=4,'feat_1'=2] {'feat_0'}, use_global_device_ids=true, to_apply=%region_8.9 | all-reduce | flops 264 | bytes 2112 | tf_op jit(solution)/shard_map/psum | solution.py:26
  145.5 4.9 %psum.39 = f32[8,33]{1,0:T(8,128)S(1)} all-reduce(f32[8,33]{1,0:T(8,128)S(1)} %psum.38), channel_id=1, replica_groups=mesh['row_0'=2,'row_1'=8,'row_2'=2,'feat_0'=4,'feat_1'=2] {'feat_1'}, use_global_device_ids=true, to_apply=%region_9.10 | all-reduce | flops 264 | bytes 2112 | tf_op jit(solution)/shard_map/psum | solution.py:26
  152.1 243.2 %all-reduce.3.cloned.1.call-done = f32[128,16896]{1,0:T(8,128)} async-done(((f32[128,16896]{1,0:T(8,128)}), f32[128,16896]{1,0:T(8,128)}) %all-reduce.3.cloned.1.call-update) | async-done | bytes 8650768
  396.5 1.1 reshape.72
  397.6 25.9 %fusion.22 = f32[4,64,8,33]{3,2,1,0:T(8,128)S(1)} fusion(f32[4,64,8,33]{3,2,1,0:T(8,128)S(1)} %reshape.72), kind=kOutput, calls=%fused_computation.39 | output fusion | flops 4257792 | bytes 540672 | tf_op jit(solution)/shard_map/jit(cumsum)/reduce_window_sum | solution.py:59
  424.7 6.4 %pmax.35 = f32[8]{0:T(128)S(1)} all-reduce(f32[8]{0:T(128)S(1)} %get-tuple-element.58), channel_id=1, replica_groups=mesh['row_0'=2,'row_1'=8,'row_2'=2,'feat_0'=4,'feat_1'=2] {'row_0'}, use_global_device_ids=true, to_apply=%region_13.14 | all-reduce | flops 8 | bytes 64 | tf_op jit(solution)/shard_map/pmax | solution.py:42
  431.2 19.9 %pmax.36 = f32[8]{0:T(128)S(1)} all-reduce(f32[8]{0:T(128)S(1)} %pmax.35), channel_id=1, replica_groups=mesh['row_0'=2,'row_1'=8,'row_2'=2,'feat_0'=4,'feat_1'=2] {'row_1'}, use_global_device_ids=true, to_apply=%region_14.15 | all-reduce | flops 8 | bytes 64 | tf_op jit(solution)/shard_map/pmax | solution.py:42
  451.1 2.5 pmax.37
  453.6 10.4 %pmax.38 = f32[8]{0:T(128)S(1)} all-reduce(f32[8]{0:T(128)S(1)} %pmax.37), channel_id=1, replica_groups=mesh['row_0'=2,'row_1'=8,'row_2'=2,'feat_0'=4,'feat_1'=2] {'feat_0'}, use_global_device_ids=true, to_apply=%region_16.17 | all-reduce | flops 8 | bytes 64 | tf_op jit(solution)/shard_map/pmax | solution.py:42
  464.7 5.4 %pmax.39 = f32[8]{0:T(128)} all-reduce(f32[8]{0:T(128)S(1)} %pmax.38), channel_id=1, replica_groups=mesh['row_0'=2,'row_1'=8,'row_2'=2,'feat_0'=4,'feat_1'=2] {'feat_1'}, use_global_device_ids=true, to_apply=%region_17.18 | all-reduce | flops 8 | bytes 64 | tf_op jit(solution)/shard_map/pmax | solution.py:42
  (76 shorter events, 36.9 us)
Async XLA Ops:
  9.3 12.6 %all-to-all-start = ((bf16[8,384,33]{1,2,0:T(8,128)(2,1)}), bf16[8,384,33]{1,2,0:T(8,128)(2,1)S(1)}, u32[]{:S(2)}, u32[]{:S(2)}) async-start(bf16[8,384,33]{1,2,0:T(8,128)(2,1)} %stack.2), calls=%async_computation | async-start | bytes 491520 | tf_op jit(solution)/shard_map/all_to_all | solution.py:21
  14.7 380.6 %all-reduce.3.cloned.1.call-start = ((), (), s32[]{:S(2)}) async-start(), calls=%async_computation.1 | async-start | bytes 17301504
  108.6 0.7 copy-start.1
  108.6 1.5 copy-start
  108.6 42.3 %copy-start.2 = (u32[256]{0:T(256)S(1)}, u32[256]{0:T(256)}, u32[]{:S(2)}) copy-start(u32[256]{0:T(256)} %constant.46) | copy-start | bytes 3076
Sparse Core Ops, SparseCore 0:
  108.8 286.5 all-reduce.2
